TPU v7x, 32 devices: a whole 2x2x4 slice. The times are simulated.
32 devices in a mesh: dp: 8 (over z, core), tp: 4 (over y, x).
Axes of the slice: x: 2, y: 2, z: 4, core: 2. Of those that a mesh axis runs over, the one named last changes fastest.
Arguments:
- student_hidden: bfloat16 [1152, 3456], P('dp'), may hold values from -6 to 6
- norm_gain: float32 [3456], replicated, may hold values from 0.25 to 1.75
- projection: bfloat16 [3456, 8192], P(None, 'tp'), may hold values from -0.109375 to 0.109375
- teacher_partials: bfloat16 [4, 1152, 8192], P('tp', 'dp'), may hold values from -5 to 5
- teacher_residual: bfloat16 [1152, 8192], P('dp', 'tp'), may hold values from -90 to 90
- owner: int32 [1152], P('dp'), may hold values from 0 to 1151, as said below
Outputs:
- grad_scaled: float32 [3456, 8192], P('dp', 'tp')
Inputs may be any that keep to these rules, and one draw needn't show every extreme that they name: owner is a permutation of all token indices; the 144 teacher rows of each index of dp hold exactly 18 tokens owned by each index of dp.
All inputs are finite; a program needn't handle non-finite values.
Results may differ from a plain program's by a relative error of at most 0.009.
Values may be sent and summed in bfloat16 or wider, within the bound.
A program may use at most 128 MiB of HBM per device.

v0:
```python
import jax
import jax.numpy as jnp
from jax import lax
from jax.sharding import PartitionSpec as P


def agree(largest):
    return lax.pmax(largest, ("dp", "tp")) + 1e-06


def rounded_terms(partial_value, scale):
    return lax.optimization_barrier((partial_value / scale).astype(jnp.bfloat16)).astype(
        jnp.float32
    )


def per_device(student_hidden, norm_gain, projection, teacher_partials, teacher_residual, owner):
    columns = projection.shape[1]
    rows_dev = student_hidden.shape[0]
    terms_in = teacher_partials[0].astype(jnp.float32)
    summed_all = lax.psum(terms_in.astype(jnp.bfloat16), "tp").astype(jnp.float32)
    summed = lax.dynamic_slice_in_dim(summed_all, lax.axis_index("tp") * columns, columns, 1)
    teacher = (teacher_residual.astype(jnp.float32) + summed).astype(jnp.bfloat16)
    groups = lax.axis_size("dp")
    slots = rows_dev // groups
    destination = owner // rows_dev
    order = jnp.argsort(destination, stable=True)
    outgoing = teacher[order].reshape(groups, slots, columns)
    outgoing_owner = owner[order].reshape(groups, slots)
    arrived, arrived_owner = (
        lax.all_to_all(outgoing, "dp", split_axis=0, concat_axis=0, tiled=True),
        lax.all_to_all(outgoing_owner, "dp", split_axis=0, concat_axis=0, tiled=True),
    )
    placing = jnp.argsort(arrived_owner.reshape(-1) % rows_dev)
    target = arrived.reshape(rows_dev, columns)[placing]
    values = student_hidden.astype(jnp.float32)
    inverse = lax.rsqrt(jnp.mean(values * values, axis=-1, keepdims=True) + 1e-05)
    normed = (values * inverse * norm_gain).astype(jnp.bfloat16)
    pred = jnp.dot(normed, projection, preferred_element_type=jnp.float32)
    diff = (pred - target.astype(jnp.float32)).astype(jnp.bfloat16)
    feature_share = normed.shape[1] // groups
    blocks = lax.all_to_all(normed, "dp", split_axis=1, concat_axis=0, tiled=True).reshape(
        groups, rows_dev, feature_share
    )
    errors = lax.all_gather(diff, "dp", axis=0, tiled=True).reshape(groups, rows_dev, columns)
    partials = jnp.einsum("dsr,dsc->drc", blocks, errors, preferred_element_type=jnp.float32)
    scale = agree(jnp.max(jnp.abs(partials)))
    grad_scaled = jnp.sum(rounded_terms(partials, scale), axis=0)
    return grad_scaled


def solution(mesh):
    placed = (P("dp", None), P(), P(None, "tp"), P("tp", "dp", None), P("dp", "tp"), P("dp"))
    return jax.shard_map(
        per_device, mesh=mesh, in_specs=placed, out_specs=P("dp", "tp"), check_vma=False
    )
```

profile of v0, /device:TPU:12, one launch (start us, length us, event | category | flops | bytes accessed | tf_op | source)
XLA Modules:
  0.0 277.4 jit_solution(12854644300265450455)
XLA Ops:
  6.5 0.0 all-reduce.2.cloned.1.call-start
  6.5 0.7 all-reduce.2.cloned.1.call-update
  7.3 0.0 copy-done
  7.3 3.2 %sort.34 = (s32[144]{0:T(256)}, s32[144]{0:T(256)S(1)}) sort(s32[144]{0:T(256)S(1)} %and_select_fusion.1, s32[144]{0:T(256)S(1)} %iota.8), dimensions={0}, to_apply=%region_2.3 | sort | flops 1152 | bytes 2304 | tf_op jit(solution)/shard_map/jit(argsort)/sort | solution.py:27
  10.5 1.6 gather_fusion.1
  12.1 0.7 all_to_all.25
  12.8 5.3 %all-to-all-start.2 = ((s32[8,1,18]{2,1,0:T(1,128)}), s32[8,1,18]{2,1,0:T(1,128)S(1)}, u32[]{:S(2)}, u32[]{:S(2)}) async-start(s32[8,1,18]{2,1,0:T(1,128)} %all_to_all.25), calls=%async_computation.2 | async-start | bytes 8192 | tf_op jit(solution)/shard_map/all_to_all | solution.py:32
  18.1 0.0 copy-done.1
  18.1 0.3 fusion.1
  18.4 66.9 %all-reduce.2.cloned.1.call-done = bf16[144,8192]{1,0:T(8,128)(2,1)} async-done(((bf16[144,8192]{1,0:T(8,128)(2,1)}), bf16[144,8192]{1,0:T(8,128)(2,1)}) %all-reduce.2.cloned.1.call-update) | async-done | bytes 2359312 | tf_op jit(solution)/shard_map/psum | solution.py:21
  85.3 1.3 add_convert_fusion
  86.6 1.0 gather_fusion
  87.6 0.0 copy-start.3
  87.6 1.1 reshape.31
  88.7 0.0 all-to-all-done.2
  88.7 5.1 %all-to-all-start.1 = ((bf16[8,18,2048]{2,1,0:T(8,128)(2,1)}), bf16[8,18,2048]{2,1,0:T(8,128)(2,1)S(1)}, u32[]{:S(2)}, u32[]{:S(2)}) async-start(bf16[8,18,2048]{2,1,0:T(8,128)(2,1)} %reshape.31), calls=%async_computation.1 | async-start | bytes 1572864 | tf_op jit(solution)/shard_map/all_to_all | solution.py:31
  93.8 0.3 fusion.3
  94.1 0.1 rem.23
  94.2 3.2 %sort.35 = (s32[144]{0:T(256)}, s32[144]{0:T(256)S(1)}) sort(s32[144]{0:T(256)S(1)} %and_select_fusion, s32[144]{0:T(256)S(1)} %iota.9), dimensions={0}, to_apply=%region_3.4 | sort | flops 1152 | bytes 2304 | tf_op jit(solution)/shard_map/jit(argsort)/sort | solution.py:34
  97.5 13.8 %all-to-all-done.1 = bf16[8,18,2048]{2,1,0:T(8,128)(2,1)S(1)} async-done(((bf16[8,18,2048]{2,1,0:T(8,128)(2,1)}), bf16[8,18,2048]{2,1,0:T(8,128)(2,1)S(1)}, u32[]{:S(2)}, u32[]{:S(2)}) %all-to-all-start.1) | async-done | bytes 589856 | tf_op jit(solution)/shard_map/all_to_all | solution.py:31
  111.3 0.2 reshape.32
  111.5 1.0 gather_fusion.2
  112.5 8.4 %fusion = bf16[144,2048]{1,0:T(8,128)(2,1)} fusion(bf16[144,3456]{1,0:T(8,128)(2,1)S(1)} %fusion.3, bf16[3456,2048]{1,0:T(8,128)(2,1)} %param.8, bf16[144,2048]{1,0:T(8,128)(2,1)S(1)} %gather_fusion.2), kind=kOutput, calls=%fused_computation.9 | convolution fusion | flops 2039316480 | bytes 16330752 | tf_op jit(solution)/shard_map/dot_general | solution.py:39
  120.9 0.0 all-gather.2.cloned.1.call-update
  120.9 2.7 all_to_all.21
  123.6 0.4 copy.7
  123.9 62.7 %all_to_all.30 = bf16[144,8,432]{2,0,1:T(8,128)(2,1)S(1)} all-to-all(bf16[144,8,432]{2,0,1:T(8,128)(2,1)S(1)} %copy.7), channel_id=1, replica_groups=mesh['dp'=8,'tp'=4] {'dp'}, dimensions={1} | all-to-all | bytes 1990656 | tf_op jit(solution)/shard_map/all_to_all | solution.py:42
  186.7 8.5 %all-gather.2.cloned.1.call-done = bf16[1152,2048]{1,0:T(8,128)(2,1)} async-done(((bf16[144,2048]{1,0:T(8,128)(2,1)}), bf16[1152,2048]{1,0:T(8,128)(2,1)}) %all-gather.2.cloned.1.call-update) | async-done | bytes 4718608 | tf_op jit(solution)/shard_map/all_gather | solution.py:45
  195.1 16.4 %abs_reduce_fusion = (f32[]{:T(128)}, f32[8,432,2048]{2,1,0:T(8,128)}) fusion(bf16[8,144,2048]{2,1,0:T(8,128)(2,1)} %bitcast.10, bf16[144,8,432]{2,0,1:T(8,128)(2,1)S(1)} %all_to_all.30), kind=kOutput, calls=%fused_computation.5 | convolution fusion | flops 2052587520 | bytes 34025476 | tf_op jit(solution)/shard_map/dsr,dsc->drc/dot_general | solution.py:46
  211.5 42.5 %pmax.7 = f32[]{:T(128)} all-reduce(f32[]{:T(128)} %get-tuple-element.9), channel_id=1, replica_groups=mesh['dp'=8,'tp'=4] {'dp','tp'}, use_global_device_ids=true, to_apply=%region_5.6 | all-reduce | flops 1 | bytes 8 | tf_op jit(solution)/shard_map/pmax | solution.py:8
  254.7 11.1 %divide_convert_fusion = bf16[8,432,2048]{2,1,0:T(8,128)(2,1)S(1)} fusion(f32[8,432,2048]{2,1,0:T(8,128)} %get-tuple-element.10, f32[]{:T(128)S(6)} %add.43), kind=kLoop, calls=%fused_computation.4 | loop fusion | flops 14155776 | bytes 42467332 | tf_op jit(solution)/shard_map/convert_element_type | solution.py:12
  265.8 4.8 %convert_reduce_fusion = f32[432,2048]{1,0:T(8,128)} fusion(bf16[8,432,2048]{2,1,0:T(8,128)(2,1)S(1)} %divide_convert_fusion), kind=kLoop, calls=%fused_computation.3 | loop fusion | flops 13271040 | bytes 17694720 | tf_op jit(solution)/shard_map/reduce_sum | solution.py:48
  (16 shorter events, 0.1 us)
Async XLA Ops:
  6.5 0.7 copy-start
  6.5 11.6 %copy-start.1 = (bf16[144,3456]{1,0:T(8,128)(2,1)S(1)}, bf16[144,3456]{1,0:T(8,128)(2,1)}, u32[]{:S(2)}) copy-start(bf16[144,3456]{1,0:T(8,128)(2,1)} %param.6) | copy-start | bytes 2985988
  6.5 78.8 %copy-start.2 = (bf16[144,2048]{1,0:T(8,128)(2,1)S(1)}, bf16[144,2048]{1,0:T(8,128)(2,1)}, u32[]{:S(2)}) copy-start(bf16[144,2048]{1,0:T(8,128)(2,1)} %param.10) | copy-start | bytes 1769476
  6.5 78.8 %all-reduce.2.cloned.1.call-start = ((), (), s32[]{:S(2)}) async-start(), calls=%async_computation.3 | async-start | bytes 4718592 | tf_op jit(solution)/shard_map/psum | solution.py:21
  12.8 75.9 %all-to-all-start.2 = ((s32[8,1,18]{2,1,0:T(1,128)}), s32[8,1,18]{2,1,0:T(1,128)S(1)}, u32[]{:S(2)}, u32[]{:S(2)}) async-start(s32[8,1,18]{2,1,0:T(1,128)} %all_to_all.25), calls=%async_computation.2 | async-start | bytes 8192 | tf_op jit(solution)/shard_map/all_to_all | solution.py:32
  87.6 6.2 %copy-start.3 = (f32[3456]{0:T(1024)S(1)}, f32[3456]{0:T(1024)}, u32[]{:S(2)}) copy-start(f32[3456]{0:T(1024)} %param.7) | copy-start | bytes 41476
  88.7 22.6 %all-to-all-start.1 = ((bf16[8,18,2048]{2,1,0:T(8,128)(2,1)}), bf16[8,18,2048]{2,1,0:T(8,128)(2,1)S(1)}, u32[]{:S(2)}, u32[]{:S(2)}) async-start(bf16[8,18,2048]{2,1,0:T(8,128)(2,1)} %reshape.31), calls=%async_computation.1 | async-start | bytes 1572864 | tf_op jit(solution)/shard_map/all_to_all | solution.py:31
  93.8 101.3 %all-gather.2.cloned.1.call-start = ((), (), s32[]{:S(2)}) async-start(), calls=%async_computation.4 | async-start | bytes 5308416 | tf_op jit(solution)/shard_map/all_gather | solution.py:45
Sparse Core Ops, SparseCore 0:
  10.5 74.8 all-reduce.1
  121.0 74.0 all-gather.1
where the time goes:
time: 278 us; the launch traced here: 277 us
  blocking collectives  105 us (38%)
  waiting for transfers between devices  90 us (32%)
  matrix products  24.7 us (9%)
  other arithmetic  24.2 us (9%)
  between operations  14.1 us (5%)
  starting transfers between devices  10.5 us (4%)
  local copies, waits for them, and re-layouts  8.65 us (3%)
    psum x1, waiting for transfers between devices, per_device(): lax.psum(terms_in.astype(jnp.bfloat16), 'tp').astype(jnp.float32)  66.9 us
    all_to_all x1, blocking collectives, per_device(): lax.all_to_all(normed, 'dp', split_axis=1, concat_axis=0, tiled=True)  62.7 us
    pmax x1, blocking collectives, agree(): return lax.pmax(largest, ('dp', 'tp')) + 1e-06  42.5 us
    dot_general x1, matrix products, per_device(): jnp.einsum('dsr,dsc->drc', blocks, errors, preferred_element_type=jnp.flo...  16.4 us
    all_to_all x1, waiting for transfers between devices, per_device(): lax.all_to_all(outgoing, 'dp', split_axis=0, concat_axis=0, tiled=True)  13.8 us
    convert_element_type x1, other arithmetic, rounded_terms(): (partial_value / scale).astype(jnp.bfloat16)  11.1 us
    all_gather x1, waiting for transfers between devices, per_device(): lax.all_gather(diff, 'dp', axis=0, tiled=True)  8.48 us
    dot_general x1, matrix products, per_device(): pred = jnp.dot(normed, projection, preferred_element_type=jnp.float32)  8.37 us
  transfers between devices with their start and end apart: 4, of which 3 were waited for; matrix products, arithmetic and copies ran while one was open for 4% of the time, Pallas kernels for 0%

commit v1 on v0

--- a/solution.py
+++ b/solution.py
@@ -18,7 +18,7 @@
     columns = projection.shape[1]
     rows_dev = student_hidden.shape[0]
     terms_in = teacher_partials[0].astype(jnp.float32)
-    summed_all = lax.psum(terms_in.astype(jnp.bfloat16), "tp").astype(jnp.float32)
+    summed_all = lax.all_gather(terms_in.astype(jnp.bfloat16), "tp").sum(axis=0).astype(jnp.float32)
     summed = lax.dynamic_slice_in_dim(summed_all, lax.axis_index("tp") * columns, columns, 1)
     teacher = (teacher_residual.astype(jnp.float32) + summed).astype(jnp.bfloat16)
     groups = lax.axis_size("dp")

time: 278 us -> 306 us (1.10)
  waiting for transfers between devices: 90 us -> 111 us
  other arithmetic: 24.2 us -> 31.6 us
    all_gather x0 -> x1, waiting for transfers between devices: none -> 88.1 us  [per_device(): lax.all_gather(terms_in.astype(jnp.bfloat16), 'tp').sum(axis=0)]
    psum x1 -> x0, waiting for transfers between devices: 66.9 us -> none  [per_device(): lax.psum(terms_in.astype(jnp.bfloat16), 'tp').astype(jnp.float32)]
    reduce_sum x0 -> x1, other arithmetic: none -> 7.52 us  [per_device(): lax.all_gather(terms_in.astype(jnp.bfloat16), 'tp').sum(axis=0)]
  transfers between devices with their start and end apart: 4 -> 4, of which waited for: 3 -> 3; matrix products, arithmetic and copies ran while one was open for 4% -> 6% of each run, Pallas kernels for 0% -> 0%
where the time goes in v1:
time: 306 us
  waiting for transfers between devices  111 us (36%)
  blocking collectives  105 us (34%)
  other arithmetic  31.6 us (10%)
  matrix products  24.7 us (8%)
  between operations  14.2 us (5%)
  starting transfers between devices  10.5 us (3%)
  local copies, waits for them, and re-layouts  8.64 us (3%)
    all_gather x1, waiting for transfers between devices, per_device(): lax.all_gather(terms_in.astype(jnp.bfloat16), 'tp').sum(axis=0)  88.1 us
    all_to_all x1, blocking collectives, per_device(): lax.all_to_all(normed, 'dp', split_axis=1, concat_axis=0, tiled=True)  62.7 us
    pmax x1, blocking collectives, agree(): return lax.pmax(largest, ('dp', 'tp')) + 1e-06  42.4 us
    dot_general x1, matrix products, per_device(): jnp.einsum('dsr,dsc->drc', blocks, errors, preferred_element_type=jnp.flo...  16.3 us
    all_to_all x1, waiting for transfers between devices, per_device(): lax.all_to_all(outgoing, 'dp', split_axis=0, concat_axis=0, tiled=True)  13.8 us
    convert_element_type x1, other arithmetic, rounded_terms(): (partial_value / scale).astype(jnp.bfloat16)  11.1 us
    all_gather x1, waiting for transfers between devices, per_device(): lax.all_gather(diff, 'dp', axis=0, tiled=True)  8.44 us
    dot_general x1, matrix products, per_device(): pred = jnp.dot(normed, projection, preferred_element_type=jnp.float32)  8.42 us
  transfers between devices with their start and end apart: 4, of which 3 were waited for; matrix products, arithmetic and copies ran while one was open for 6% of the time, Pallas kernels for 0%

profile of v1, /device:TPU:12, one launch (start us, length us, event | category | flops | bytes accessed | tf_op | source)
XLA Modules:
  0.0 305.8 jit_solution(1552817123931303720)
XLA Ops:
  6.5 0.0 all-gather.3.cloned.1.call-start
  6.5 0.7 all-gather.3.cloned.1.call-update
  7.3 3.2 %sort.34 = (s32[144]{0:T(256)}, s32[144]{0:T(256)S(1)}) sort(s32[144]{0:T(256)S(1)} %and_select_fusion.1, s32[144]{0:T(256)S(1)} %iota.8), dimensions={0}, to_apply=%region_2.3 | sort | flops 1152 | bytes 2304 | tf_op jit(solution)/shard_map/jit(argsort)/sort | solution.py:27
  10.5 1.6 gather_fusion.1
  12.1 0.7 all_to_all.25
  12.8 5.3 %all-to-all-start.2 = ((s32[8,1,18]{2,1,0:T(1,128)}), s32[8,1,18]{2,1,0:T(1,128)S(1)}, u32[]{:S(2)}, u32[]{:S(2)}) async-start(s32[8,1,18]{2,1,0:T(1,128)} %all_to_all.25), calls=%async_computation.2 | async-start | bytes 8192 | tf_op jit(solution)/shard_map/all_to_all | solution.py:32
  18.1 0.3 fusion.1
  18.4 88.1 %all-gather.3.cloned.1.call-done = bf16[4,144,8192]{2,1,0:T(8,128)(2,1)} async-done(((bf16[1,144,8192]{2,1,0:T(8,128)(2,1)}), bf16[4,144,8192]{2,1,0:T(8,128)(2,1)}) %all-gather.3.cloned.1.call-update) | async-done | bytes 9437200 | tf_op jit(solution)/shard_map/all_gather | solution.py:21
  106.5 7.5 %reduce_sum.31 = bf16[144,8192]{1,0:T(8,128)(2,1)} reduce(bf16[4,144,8192]{2,1,0:T(8,128)(2,1)} %all-gather.3.cloned.1.call-done, bf16[]{:T(256)} %constant.18.clone.1), dimensions={0}, to_apply=%region_1.2 | reduce | flops 3538944 | bytes 11796482 | tf_op jit(solution)/shard_map/reduce_sum | solution.py:21
  114.0 0.0 copy-done.2
  114.0 1.2 add_convert_fusion
  115.3 1.0 gather_fusion
  116.2 0.0 copy-start.3
  116.3 1.1 reshape.32
  117.3 0.0 all-to-all-done.2
  117.3 5.1 %all-to-all-start.1 = ((bf16[8,18,2048]{2,1,0:T(8,128)(2,1)}), bf16[8,18,2048]{2,1,0:T(8,128)(2,1)S(1)}, u32[]{:S(2)}, u32[]{:S(2)}) async-start(bf16[8,18,2048]{2,1,0:T(8,128)(2,1)} %reshape.32), calls=%async_computation.1 | async-start | bytes 1572864 | tf_op jit(solution)/shard_map/all_to_all | solution.py:31
  122.5 0.3 fusion.3
  122.8 0.1 rem.23
  122.9 3.2 %sort.35 = (s32[144]{0:T(256)}, s32[144]{0:T(256)S(1)}) sort(s32[144]{0:T(256)S(1)} %and_select_fusion, s32[144]{0:T(256)S(1)} %iota.9), dimensions={0}, to_apply=%region_3.4 | sort | flops 1152 | bytes 2304 | tf_op jit(solution)/shard_map/jit(argsort)/sort | solution.py:34
  126.1 13.8 %all-to-all-done.1 = bf16[8,18,2048]{2,1,0:T(8,128)(2,1)S(1)} async-done(((bf16[8,18,2048]{2,1,0:T(8,128)(2,1)}), bf16[8,18,2048]{2,1,0:T(8,128)(2,1)S(1)}, u32[]{:S(2)}, u32[]{:S(2)}) %all-to-all-start.1) | async-done | bytes 589856 | tf_op jit(solution)/shard_map/all_to_all | solution.py:31
  140.0 0.2 reshape.33
  140.1 1.0 gather_fusion.2
  141.1 8.4 %fusion = bf16[144,2048]{1,0:T(8,128)(2,1)} fusion(bf16[144,3456]{1,0:T(8,128)(2,1)S(1)} %fusion.3, bf16[3456,2048]{1,0:T(8,128)(2,1)} %param.8, bf16[144,2048]{1,0:T(8,128)(2,1)S(1)} %gather_fusion.2), kind=kOutput, calls=%fused_computation.9 | convolution fusion | flops 2039316480 | bytes 16330752 | tf_op jit(solution)/shard_map/dot_general | solution.py:39
  149.6 0.0 all-gather.5.cloned.1.call-update
  149.6 2.7 all_to_all.21
  152.3 0.4 copy.8
  152.6 62.7 %all_to_all.30 = bf16[144,8,432]{2,0,1:T(8,128)(2,1)S(1)} all-to-all(bf16[144,8,432]{2,0,1:T(8,128)(2,1)S(1)} %copy.8), channel_id=1, replica_groups=mesh['dp'=8,'tp'=4] {'dp'}, dimensions={1} | all-to-all | bytes 1990656 | tf_op jit(solution)/shard_map/all_to_all | solution.py:42
  215.3 8.4 %all-gather.5.cloned.1.call-done = bf16[1152,2048]{1,0:T(8,128)(2,1)} async-done(((bf16[144,2048]{1,0:T(8,128)(2,1)}), bf16[1152,2048]{1,0:T(8,128)(2,1)}) %all-gather.5.cloned.1.call-update) | async-done | bytes 4718608 | tf_op jit(solution)/shard_map/all_gather | solution.py:45
  223.8 16.3 %abs_reduce_fusion = (f32[]{:T(128)}, f32[8,432,2048]{2,1,0:T(8,128)}) fusion(bf16[8,144,2048]{2,1,0:T(8,128)(2,1)} %bitcast.9, bf16[144,8,432]{2,0,1:T(8,128)(2,1)S(1)} %all_to_all.30), kind=kOutput, calls=%fused_computation.5 | convolution fusion | flops 2052587520 | bytes 34025476 | tf_op jit(solution)/shard_map/dsr,dsc->drc/dot_general | solution.py:46
  240.1 42.4 %pmax.7 = f32[]{:T(128)} all-reduce(f32[]{:T(128)} %get-tuple-element.9), channel_id=1, replica_groups=mesh['dp'=8,'tp'=4] {'dp','tp'}, use_global_device_ids=true, to_apply=%region_5.6 | all-reduce | flops 1 | bytes 8 | tf_op jit(solution)/shard_map/pmax | solution.py:8
  283.2 11.1 %divide_convert_fusion = bf16[8,432,2048]{2,1,0:T(8,128)(2,1)S(1)} fusion(f32[8,432,2048]{2,1,0:T(8,128)} %get-tuple-element.10, f32[]{:T(128)S(6)} %add.41), kind=kLoop, calls=%fused_computation.4 | loop fusion | flops 14155776 | bytes 42467332 | tf_op jit(solution)/shard_map/convert_element_type | solution.py:12
  294.3 4.7 %convert_reduce_fusion = f32[432,2048]{1,0:T(8,128)} fusion(bf16[8,432,2048]{2,1,0:T(8,128)(2,1)S(1)} %divide_convert_fusion), kind=kLoop, calls=%fused_computation.3 | loop fusion | flops 13271040 | bytes 17694720 | tf_op jit(solution)/shard_map/reduce_sum | solution.py:48
  (17 shorter events, 0.1 us)
Async XLA Ops:
  6.5 0.7 copy-start
  6.5 11.6 %copy-start.1 = (bf16[144,3456]{1,0:T(8,128)(2,1)S(1)}, bf16[144,3456]{1,0:T(8,128)(2,1)}, u32[]{:S(2)}) copy-start(bf16[144,3456]{1,0:T(8,128)(2,1)} %param.6) | copy-start | bytes 2985988
  6.5 100.0 %all-gather.3.cloned.1.call-start = ((), (), s32[]{:S(2)}) async-start(), calls=%async_computation.3 | async-start | bytes 11796480 | tf_op jit(solution)/shard_map/all_gather | solution.py:21
  12.8 104.5 %all-to-all-start.2 = ((s32[8,1,18]{2,1,0:T(1,128)}), s32[8,1,18]{2,1,0:T(1,128)S(1)}, u32[]{:S(2)}, u32[]{:S(2)}) async-start(s32[8,1,18]{2,1,0:T(1,128)} %all_to_all.25), calls=%async_computation.2 | async-start | bytes 8192 | tf_op jit(solution)/shard_map/all_to_all | solution.py:32
  18.4 95.6 %copy-start.2 = (bf16[144,2048]{1,0:T(8,128)(2,1)S(1)}, bf16[144,2048]{1,0:T(8,128)(2,1)}, u32[]{:S(2)}) copy-start(bf16[144,2048]{1,0:T(8,128)(2,1)} %param.10) | copy-start | bytes 1769476
  116.2 6.2 %copy-start.3 = (f32[3456]{0:T(1024)S(1)}, f32[3456]{0:T(1024)}, u32[]{:S(2)}) copy-start(f32[3456]{0:T(1024)} %param.7) | copy-start | bytes 41476
  117.3 22.6 %all-to-all-start.1 = ((bf16[8,18,2048]{2,1,0:T(8,128)(2,1)}), bf16[8,18,2048]{2,1,0:T(8,128)(2,1)S(1)}, u32[]{:S(2)}, u32[]{:S(2)}) async-start(bf16[8,18,2048]{2,1,0:T(8,128)(2,1)} %reshape.32), calls=%async_computation.1 | async-start | bytes 1572864 | tf_op jit(solution)/shard_map/all_to_all | solution.py:31
  122.5 101.3 %all-gather.5.cloned.1.call-start = ((), (), s32[]{:S(2)}) async-start(), calls=%async_computation.4 | async-start | bytes 5308416 | tf_op jit(solution)/shard_map/all_gather | solution.py:45
Sparse Core Ops, SparseCore 0:
  9.2 97.2 all-gather.2
  149.7 74.0 all-gather.4
